TPU v7x, 128 devices: a whole 4x4x4 slice. The times are simulated.
128 devices in a mesh: frag: 4 (over y_hi, core), aux: 16 (over z, x), orb: 2 (over y_lo).
Axes of the slice: x: 4, y: 4 (y_hi: 2, y_lo: 2; y = y_hi * 2 + y_lo), z: 4, core: 2. Of those that a mesh axis runs over, the one named last changes fastest.
Arguments:
- density: bfloat16 [16384, 2, 8192], P('frag', 'orb', 'aux'), may hold values from -0.046875 to 0.046875
- bath: bfloat16 [16, 2, 8192, 128], P('frag', 'orb', 'aux'), may hold values from -1 to 1
- factor: bfloat16 [16384, 16384], P('orb', 'aux'), may hold values from -6 to 6
- frag_index: int32 [16, 128], replicated, may hold values from 0 to 16383, as said below
- nfrag: int32 [16], replicated, may hold values from 1 to 128
- nbath: int32 [16], replicated, may hold values from 1 to 128
Outputs:
- projected: bfloat16 [16, 256, 16384], P('frag', 'orb', 'aux')
Inputs may be any that keep to these rules, and one draw needn't show every extreme that they name: `frag_index`: the 128 entries of one fragment's row are distinct basis functions; entries at or past nfrag are not read.
All inputs are finite; a program needn't handle non-finite values.
Results may differ from a plain program's by a relative error of at most 0.0049.
Values may be sent and summed in bfloat16 or wider, within the bound.
A program may use at most 128 MiB of HBM per device.

v0:
```python
import jax
import jax.numpy as jnp
from jax import lax
from jax.sharding import PartitionSpec as P


def per_device(density, bath, factor, frag_index, nfrag, nbath):
    local_rows = density.shape[0]
    block_cols = density.shape[2]
    density_local = density.reshape(local_rows, block_cols)
    group_size = bath.shape[0]
    frag_max = frag_index.shape[1]
    bath_max = bath.shape[3]
    frag_count = frag_index.shape[0]
    row_offset = lax.axis_index("frag") * local_rows
    local_index = frag_index - row_offset
    owned_rows = (local_index >= 0) & (local_index < local_rows)
    picked = jnp.take(density_local, jnp.clip(local_index, 0, local_rows - 1).reshape(-1), axis=0)
    picked = picked.reshape(frag_count, frag_max, block_cols)
    picked = jnp.where(owned_rows[:, :, None], picked, jnp.zeros_like(picked))
    gathered_rows = (
        lax.psum_scatter(picked, "frag", scatter_dimension=0, tiled=True)
        .astype(jnp.float32)
        .astype(jnp.bfloat16)
    )
    first_frag = lax.axis_index("frag") * group_size
    my_nfrag = lax.dynamic_slice_in_dim(nfrag, first_frag, group_size)
    my_nbath = lax.dynamic_slice_in_dim(nbath, first_frag, group_size)
    frag_live = jnp.arange(frag_max, dtype=jnp.int32)[None, :] < my_nfrag[:, None]
    bath_live = jnp.arange(bath_max, dtype=jnp.int32)[None, :] < my_nbath[:, None]
    gathered_rows = jnp.where(frag_live[:, :, None], gathered_rows, jnp.zeros_like(gathered_rows))
    bath_cols = bath.reshape(group_size, block_cols, bath_max)
    bath_cols = jnp.where(bath_live[:, None, :], bath_cols, jnp.zeros_like(bath_cols))
    initial = jnp.concatenate([jnp.swapaxes(gathered_rows, 1, 2), bath_cols], axis=2)
    live_cols = jnp.concatenate([frag_live, bath_live], axis=1).astype(jnp.float32)
    kmax_cols = initial.shape[2]
    identity_pad = jnp.eye(kmax_cols, dtype=jnp.float32)[None] * (1.0 - live_cols)[:, :, None]
    gram_part = jnp.einsum("fmk,fml->fkl", initial, initial, preferred_element_type=jnp.float32)
    gram_total = lax.psum(gram_part, ("aux", "orb")) + identity_pad
    cholesky_low = jnp.linalg.cholesky(gram_total)
    coeffs = lax.linalg.triangular_solve(
        cholesky_low, initial.astype(jnp.float32), left_side=False, lower=True, transpose_a=True
    )
    coeffs = coeffs.astype(jnp.bfloat16)
    partial_value = jnp.einsum(
        "fmk,mq->fkq",
        lax.all_gather(coeffs, "aux", axis=1, tiled=True),
        factor,
        preferred_element_type=jnp.float32,
    )
    summed = lax.psum_scatter(partial_value, "orb", scatter_dimension=1, tiled=True)
    return summed.astype(jnp.bfloat16)


def solution(mesh):
    placed = (
        P("frag", "orb", "aux"),
        P("frag", "orb", "aux", None),
        P("orb", "aux"),
        P(),
        P(),
        P(),
    )
    return jax.shard_map(
        per_device, mesh=mesh, in_specs=placed, out_specs=P("frag", "orb", "aux"), check_vma=False
    )
```

profile of v0, /device:TPU:1, one launch (start us, length us, event | category | flops | bytes accessed | tf_op | source)
XLA Modules:
  0.0 812.8 jit_solution(12678690382864565310)
XLA Ops:
  6.5 0.7 compare_and_fusion
  7.3 10.3 %gather_fusion = bf16[2048,512]{1,0:T(8,128)(2,1)S(1)} fusion(bf16[4096,512]{1,0:T(8,128)(2,1)} %bitcast.50, s32[2048]{0:T(1024)S(1)} %broadcast_clamp_fusion), kind=kCustom, calls=%fused_computation | custom fusion | bytes 4202496 | tf_op jit(solution)/shard_map/jit(_take)/gather | solution.py:18
  17.6 2.4 copy.24
  20.0 3.2 select_select_fusion
  24.3 40.2 %reduce-scatter.3.cloned.1.call-done = bf16[4,128,512]{1,2,0:T(8,128)(2,1)} async-done(((bf16[16,128,512]{1,2,0:T(8,128)(2,1)}), bf16[4,128,512]{1,2,0:T(8,128)(2,1)}) %reduce-scatter.3.cloned.1.call-update) | async-done | bytes 524304 | tf_op jit(solution)/shard_map/reduce_scatter | solution.py:22
  64.5 1.1 fusion.8
  65.6 1.5 fusion.2
  67.5 286.9 %all-reduce.3.cloned.1.call-done = f32[4,256,256]{1,2,0:T(8,128)} async-done(((f32[4,256,256]{1,2,0:T(8,128)}), f32[4,256,256]{1,2,0:T(8,128)}) %all-reduce.3.cloned.1.call-update) | async-done | bytes 1048592 | tf_op jit(solution)/shard_map/psum | solution.py:39
  354.4 1.4 multiply_add_fusion
  356.4 46.9 %custom-call.16 = f32[4,128,128]{2,1,0:T(8,128)S(1)} custom-call(f32[4,128,128]{2,1,0:T(8,128)S(1)} %cholesky.122), custom_call_target="Cholesky" | custom-call | tf_op jit(solution)/shard_map/jit(cholesky)/cholesky | solution.py:40
  403.3 39.3 %custom-call.17 = f32[4,1,128,128]{2,3,1,0:T(8,128)S(1)} custom-call(f32[4,1,128,128]{3,2,1,0:T(8,128)S(1)} %select_bitcast_fusion), custom_call_target="InvertDiagBlocksLowerTriangular" | custom-call | tf_op jit(solution)/shard_map/jit(cholesky)/cholesky | solution.py:40
  443.1 0.7 convolution_subtract_fusion.1
  443.8 46.9 %custom-call.18 = f32[4,128,128]{2,1,0:T(8,128)S(1)} custom-call(f32[4,128,128]{2,1,0:T(8,128)S(1)} %convolution_subtract_fusion.1), custom_call_target="Cholesky" | custom-call | tf_op jit(solution)/shard_map/jit(cholesky)/cholesky | solution.py:40
  491.3 5.4 while.1
  491.9 2.1 bitcast_dynamic-update-slice_fusion.2
  494.6 2.1 bitcast_dynamic-update-slice_fusion.2
  496.7 79.4 %custom-call.19 = f32[4,2,128,128]{2,3,1,0:T(8,128)S(1)} custom-call(f32[4,2,128,128]{3,2,1,0:T(8,128)} %bitcast.54), custom_call_target="InvertDiagBlocksLowerTriangular" | custom-call | tf_op jit(solution)/shard_map/triangular_solve | solution.py:41
  576.8 1.8 convolution_subtract_fusion
  578.6 1.1 convolution_convert_fusion
  579.7 1.0 pad_maximum_fusion
  580.8 141.7 %all-gather.2.cloned.1.call-done = bf16[4,8192,256]{1,2,0:T(8,128)(2,1)} async-done(((bf16[4,512,256]{1,2,0:T(8,128)(2,1)}), bf16[4,8192,256]{1,2,0:T(8,128)(2,1)}) %all-gather.2.cloned.1.call-update) | async-done | bytes 16777232 | tf_op jit(solution)/shard_map/all_gather | solution.py:47
  722.5 23.5 %fusion = f32[4,256,1024]{2,1,0:T(8,128)} fusion(bf16[4,8192,256]{1,2,0:T(8,128)(2,1)} %all-gather.2.cloned.1.call-done, bf16[8192,1024]{1,0:T(8,128)(2,1)} %param.8), kind=kOutput, calls=%fused_computation.3 | convolution fusion | flops 17179869184 | bytes 37748736 | tf_op jit(solution)/shard_map/fmk,mq->fkq/dot_general | solution.py:45
  746.0 57.5 %reduce-scatter.5.cloned.1.call-done = f32[4,128,1024]{2,1,0:T(8,128)} async-done(((f32[4,256,1024]{2,1,0:T(8,128)}), f32[4,128,1024]{2,1,0:T(8,128)}) %reduce-scatter.5.cloned.1.call-update) | async-done | bytes 2097168 | tf_op jit(solution)/shard_map/reduce_scatter | solution.py:51
  803.5 2.7 convert_element_type.23
  (52 shorter events, 4.9 us)
Async XLA Ops:
  6.5 58.0 %reduce-scatter.3.cloned.1.call-start = ((), (), s32[]{:S(2)}) async-start(), calls=%async_computation.2 | async-start | bytes 2621440 | tf_op jit(solution)/shard_map/reduce_scatter | solution.py:22
  23.2 0.7 copy-start.5
  23.2 0.7 copy-start.6
  23.2 1.1 copy-start.4
  23.2 331.2 %all-reduce.3.cloned.1.call-start = ((), (), s32[]{:S(2)}) async-start(), calls=%async_computation.3 | async-start | bytes 2097152 | tf_op jit(solution)/shard_map/psum | solution.py:39
  24.3 42.8 %copy-start.2 = (bf16[4,512,128]{2,1,0:T(8,128)(2,1)}, bf16[4,512,128]{2,1,0:T(8,128)(2,1)S(1)}, u32[]{:S(2)}) copy-start(bf16[4,512,128]{2,1,0:T(8,128)(2,1)S(1)} %bitcast_select_fusion) | copy-start | bytes 1572868
  67.1 655.4 %all-gather.2.cloned.1.call-start = ((), (), s32[]{:S(2)}) async-start(), calls=%async_computation.4 | async-start | bytes 17825792 | tf_op jit(solution)/shard_map/all_gather | solution.py:47
  354.4 1.8 copy-start
  491.0 85.1 %copy-start.1 = (bf16[4,128,512]{1,2,0:T(8,128)(2,1)S(1)}, bf16[4,128,512]{1,2,0:T(8,128)(2,1)}, u32[]{:S(2)}) copy-start(bf16[4,128,512]{1,2,0:T(8,128)(2,1)} %reduce-scatter.3.cloned.1.call-done) | copy-start | bytes 1572868
  491.3 85.5 %copy-start.3 = (bf16[4,512,128]{2,1,0:T(8,128)(2,1)S(1)}, bf16[4,512,128]{2,1,0:T(8,128)(2,1)}, u32[]{:S(2)}) copy-start(bf16[4,512,128]{2,1,0:T(8,128)(2,1)} %copy-done.2) | copy-start | bytes 1572868
  580.7 222.8 %reduce-scatter.5.cloned.1.call-start = ((), (), s32[]{:S(2)}) async-start(), calls=%async_computation.5 | async-start | bytes 6291456 | tf_op jit(solution)/shard_map/reduce_scatter | solution.py:51
Sparse Core Ops, SparseCore 0:
  23.3 41.1 reduce-scatter.2
  67.2 287.1 all-reduce.2
  580.9 141.6 all-gather.1
  746.2 57.3 reduce-scatter.4
where the time goes:
time: 813 us
  waiting for transfers between devices  526 us (65%)
  other arithmetic  224 us (28%)
  matrix products  29.6 us (4%)
  local copies, waits for them, and re-layouts  19.5 us (2%)
  between operations  13.4 us (2%)
    psum x1, waiting for transfers between devices, per_device(): gram_total = lax.psum(gram_part, ('aux', 'orb')) + identity_pad  287 us
    all_gather x1, waiting for transfers between devices, per_device(): lax.all_gather(coeffs, 'aux', axis=1, tiled=True)  142 us
    another operation x10, other arithmetic, per_device(): cholesky_low = jnp.linalg.cholesky(gram_total)  133 us
    another operation x5, other arithmetic, per_device(): lax.linalg.triangular_solve(cholesky_low, initial.astype(jnp.float32), le...  80.7 us
    reduce_scatter x1, waiting for transfers between devices, per_device(): lax.psum_scatter(partial_value, 'orb', scatter_dimension=1, tiled=True)  57.5 us
    reduce_scatter x1, waiting for transfers between devices, per_device(): lax.psum_scatter(picked, 'frag', scatter_dimension=0, tiled=True)  40.2 us
    dot_general x1, matrix products, per_device(): jnp.einsum('fmk,mq->fkq', lax.all_gather(coeffs, 'aux', axis=1, tiled=Tru...  23.5 us
  transfers between devices with their start and end apart: 4, of which 4 were waited for; matrix products, arithmetic and copies ran while one was open for 0% of the time, Pallas kernels for 0%

commit v1 on v0

--- a/solution.py
+++ b/solution.py
@@ -2,6 +2,10 @@
 import jax.numpy as jnp
 from jax import lax
 from jax.sharding import PartitionSpec as P
+
+
+def save_the_clusters(x_in):
+    return lax.all_gather(x_in, ("aux", "orb")).sum(axis=0)
 
 
 def per_device(density, bath, factor, frag_index, nfrag, nbath):
@@ -36,7 +40,7 @@
     kmax_cols = initial.shape[2]
     identity_pad = jnp.eye(kmax_cols, dtype=jnp.float32)[None] * (1.0 - live_cols)[:, :, None]
     gram_part = jnp.einsum("fmk,fml->fkl", initial, initial, preferred_element_type=jnp.float32)
-    gram_total = lax.psum(gram_part, ("aux", "orb")) + identity_pad
+    gram_total = save_the_clusters(gram_part) + identity_pad
     cholesky_low = jnp.linalg.cholesky(gram_total)
     coeffs = lax.linalg.triangular_solve(
         cholesky_low, initial.astype(jnp.float32), left_side=False, lower=True, transpose_a=True

time: 813 us -> 1230 us (1.51)
  waiting for transfers between devices: 526 us -> 933 us
    all_gather x0 -> x1, waiting for transfers between devices: none -> 707 us  [save_the_clusters(): return lax.all_gather(x_in, ('aux', 'orb')).sum(axis=0)]
    psum x1 -> x0, waiting for transfers between devices: 287 us -> none  [per_device(): gram_total = lax.psum(gram_part, ('aux', 'orb')) + identity_pad]
    all_gather x1, waiting for transfers between devices: 142 us -> 128 us  [per_device(): lax.all_gather(coeffs, 'aux', axis=1, tiled=True)]
where the time goes in v1:
time: 1230 us
  waiting for transfers between devices  933 us (76%)
  other arithmetic  236 us (19%)
  matrix products  29.6 us (2%)
  local copies, waits for them, and re-layouts  19.7 us (2%)
  between operations  13.4 us (1%)
    all_gather x1, waiting for transfers between devices, save_the_clusters(): return lax.all_gather(x_in, ('aux', 'orb')).sum(axis=0)  707 us
    another operation x10, other arithmetic, per_device(): cholesky_low = jnp.linalg.cholesky(gram_total)  133 us
    all_gather x1, waiting for transfers between devices, per_device(): lax.all_gather(coeffs, 'aux', axis=1, tiled=True)  128 us
    another operation x5, other arithmetic, per_device(): lax.linalg.triangular_solve(cholesky_low, initial.astype(jnp.float32), le...  80.7 us
    reduce_scatter x1, waiting for transfers between devices, per_device(): lax.psum_scatter(partial_value, 'orb', scatter_dimension=1, tiled=True)  57.5 us
    reduce_scatter x1, waiting for transfers between devices, per_device(): lax.psum_scatter(picked, 'frag', scatter_dimension=0, tiled=True)  40.2 us
  transfers between devices with their start and end apart: 4, of which 4 were waited for; matrix products, arithmetic and copies ran while one was open for 0% of the time, Pallas kernels for 0%

profile of v1, /device:TPU:1, one launch (start us, length us, event | category | flops | bytes accessed | tf_op | source)
XLA Modules:
  0.0 1231.9 jit_solution(226728826755738780)
XLA Ops:
  7.3 10.3 gather_fusion
  17.6 2.4 copy.32
  20.0 3.2 select_select_fusion
  24.3 40.2 %reduce-scatter.3.cloned.1.call-done = bf16[4,128,512]{1,2,0:T(8,128)(2,1)} async-done(((bf16[16,128,512]{1,2,0:T(8,128)(2,1)}), bf16[4,128,512]{1,2,0:T(8,128)(2,1)}) %reduce-scatter.3.cloned.1.call-update) | async-done | bytes 524304 | tf_op jit(solution)/shard_map/reduce_scatter | solution.py:26
  64.5 1.1 fusion.9
  65.6 1.5 fusion.2
  67.3 0.7 fusion.15
  68.0 707.2 %all-gather.6.cloned.1.call-done = f32[128,256,256]{2,1,0:T(8,128)} async-done(((f32[4,256,256]{2,1,0:T(8,128)}), f32[128,256,256]{2,1,0:T(8,128)}) %all-gather.6.cloned.1.call-update) | async-done | bytes 33554448 | tf_op jit(solution)/shard_map/all_gather | solution.py:8
  775.2 12.1 reduce_sum.11
  787.7 1.2 fusion.7
  788.9 46.9 %custom-call.16 = f32[4,128,128]{2,1,0:T(8,128)S(1)} custom-call(f32[4,128,128]{2,1,0:T(8,128)S(1)} %cholesky.122), custom_call_target="Cholesky" | custom-call | tf_op jit(solution)/shard_map/jit(cholesky)/cholesky | solution.py:44
  836.0 39.3 %custom-call.17 = f32[4,1,128,128]{2,3,1,0:T(8,128)S(1)} custom-call(f32[4,1,128,128]{3,2,1,0:T(8,128)S(1)} %select_bitcast_fusion), custom_call_target="InvertDiagBlocksLowerTriangular" | custom-call | tf_op jit(solution)/shard_map/jit(cholesky)/cholesky | solution.py:44
  876.4 46.9 %custom-call.18 = f32[4,128,128]{2,1,0:T(8,128)S(1)} custom-call(f32[4,128,128]{2,1,0:T(8,128)S(1)} %convolution_subtract_fusion.1), custom_call_target="Cholesky" | custom-call | tf_op jit(solution)/shard_map/jit(cholesky)/cholesky | solution.py:44
  923.8 5.6 while.1
  924.4 2.2 bitcast_dynamic-update-slice_fusion.2
  927.2 2.2 bitcast_dynamic-update-slice_fusion.2
  929.4 79.4 %custom-call.19 = f32[4,2,128,128]{2,3,1,0:T(8,128)S(1)} custom-call(f32[4,2,128,128]{3,2,1,0:T(8,128)} %bitcast.58), custom_call_target="InvertDiagBlocksLowerTriangular" | custom-call | tf_op jit(solution)/shard_map/triangular_solve | solution.py:45
  1009.5 1.8 convolution_subtract_fusion
  1011.3 1.1 convolution_convert_fusion
  1012.4 1.0 pad_maximum_fusion
  1013.5 128.1 %all-gather.4.cloned.1.call-done = bf16[4,8192,256]{1,2,0:T(8,128)(2,1)} async-done(((bf16[4,512,256]{1,2,0:T(8,128)(2,1)}), bf16[4,8192,256]{1,2,0:T(8,128)(2,1)}) %all-gather.4.cloned.1.call-update) | async-done | bytes 16777232 | tf_op jit(solution)/shard_map/all_gather | solution.py:51
  1141.6 23.5 %fusion = f32[4,256,1024]{2,1,0:T(8,128)} fusion(bf16[4,8192,256]{1,2,0:T(8,128)(2,1)} %all-gather.4.cloned.1.call-done, bf16[8192,1024]{1,0:T(8,128)(2,1)} %param.8), kind=kOutput, calls=%fused_computation.3 | convolution fusion | flops 17179869184 | bytes 37748736 | tf_op jit(solution)/shard_map/fmk,mq->fkq/dot_general | solution.py:49
  1165.2 57.5 %reduce-scatter.5.cloned.1.call-done = f32[4,128,1024]{2,1,0:T(8,128)} async-done(((f32[4,256,1024]{2,1,0:T(8,128)}), f32[4,128,1024]{2,1,0:T(8,128)}) %reduce-scatter.5.cloned.1.call-update) | async-done | bytes 2097168 | tf_op jit(solution)/shard_map/reduce_scatter | solution.py:55
  1222.7 2.7 convert_element_type.27
  (50 shorter events, 5.9 us)
Async XLA Ops:
  6.5 58.0 %reduce-scatter.3.cloned.1.call-start = ((), (), s32[]{:S(2)}) async-start(), calls=%async_computation.2 | async-start | bytes 2621440 | tf_op jit(solution)/shard_map/reduce_scatter | solution.py:26
  23.2 0.7 copy-start.4
  23.2 0.7 copy-start.5
  23.2 1.1 copy-start.3
  23.2 752.0 %all-gather.6.cloned.1.call-start = ((), (), s32[]{:S(2)}) async-start(), calls=%async_computation.5 | async-start | bytes 34603008 | tf_op jit(solution)/shard_map/all_gather | solution.py:8
  24.3 42.8 %copy-start.1 = (bf16[4,512,128]{2,1,0:T(8,128)(2,1)}, bf16[4,512,128]{2,1,0:T(8,128)(2,1)S(1)}, u32[]{:S(2)}) copy-start(bf16[4,512,128]{2,1,0:T(8,128)(2,1)S(1)} %bitcast_select_fusion) | copy-start | bytes 1572868
  67.1 1074.5 %all-gather.4.cloned.1.call-start = ((), (), s32[]{:S(2)}) async-start(), calls=%async_computation.3 | async-start | bytes 17825792 | tf_op jit(solution)/shard_map/all_gather | solution.py:51
  923.6 85.3 %copy-start = (bf16[4,128,512]{1,2,0:T(8,128)(2,1)S(1)}, bf16[4,128,512]{1,2,0:T(8,128)(2,1)}, u32[]{:S(2)}) copy-start(bf16[4,128,512]{1,2,0:T(8,128)(2,1)} %reduce-scatter.3.cloned.1.call-done) | copy-start | bytes 1572868
  923.8 85.6 %copy-start.2 = (bf16[4,512,128]{2,1,0:T(8,128)(2,1)S(1)}, bf16[4,512,128]{2,1,0:T(8,128)(2,1)}, u32[]{:S(2)}) copy-start(bf16[4,512,128]{2,1,0:T(8,128)(2,1)} %copy-done.1) | copy-start | bytes 1572868
  1013.5 209.2 %reduce-scatter.5.cloned.1.call-start = ((), (), s32[]{:S(2)}) async-start(), calls=%async_computation.4 | async-start | bytes 6291456 | tf_op jit(solution)/shard_map/reduce_scatter | solution.py:55
Sparse Core Ops, SparseCore 0:
  23.3 41.1 reduce-scatter.2
  67.2 707.9 all-gather.5
  1013.6 128.0 all-gather.3
  1165.3 57.3 reduce-scatter.4
